TPU v7x, 256 devices: a whole 4x4x8 slice. The times are simulated.
256 devices in a mesh: seq: 64 (over x, y_lo, z), ch: 4 (over y_hi, core).
Axes of the slice: x: 4, y: 4 (y_hi: 2, y_lo: 2; y = y_hi * 2 + y_lo), z: 8, core: 2. Of those that a mesh axis runs over, the one named last changes fastest.
Arguments:
- projected: bfloat16 [8192, 3, 4096], P('seq', None, 'ch'), may hold values from -6 to 6
- cotangent: bfloat16 [8192, 4096], P('seq', 'ch'), may hold values from -6 to 6
- short_weight: float32 [3, 7, 4096], P(None, None, 'ch'), may hold values from -2 to 2
- long_filter: float32 [8, 8192], P('ch', 'seq'), may hold values from -0.0625 to 0.0625
Outputs:
- grad_proj: bfloat16 [8192, 3, 4096], P('seq', None, 'ch')
- grad_short: float32 [3, 7, 4096], P(None, None, 'ch')
- grad_filter: float32 [8, 8192], P(None, ('seq', 'ch'))
All inputs are finite; a program needn't handle non-finite values.
Results may differ from a plain program's by a relative error of at most 0.00155.
Values may be sent and summed in bfloat16 or wider, within the bound.
No kernel may reach another device: no remote copies, remote signals or barrier semaphores. Data moves between devices by JAX's collectives and lax.ppermute only.
A program may use at most 64 MiB of HBM per device.

v0:
```python
import math
import jax
import jax.numpy as jnp
from jax import lax
from jax.sharding import PartitionSpec as P

highest = lax.Precision.HIGHEST


def passed_along(block, axis, distance):
    devices = range(lax.axis_size(axis))
    route = [(i - distance, i) for i in devices if i - distance in devices]
    return lax.ppermute(block, axis, route)


def einsum_high(form, table, operand):
    return jnp.einsum(form, table, operand, precision=highest)


def angle_table(first, second, length):
    product = first[:, None] * second[None, :] % length
    radians = product.astype(jnp.float32) * (2.0 * math.pi / length)
    return (jnp.cos(radians), jnp.sin(radians))


def complex_dft(cosine, sine, real_part, imag_part, joined, sign):
    table = jnp.stack(
        [jnp.stack([cosine, -sign * sine], 0), jnp.stack([sign * sine, cosine], 0)], 0
    )
    stacked = jnp.stack([real_part, imag_part], 0)
    result = jnp.einsum(joined, table, stacked, precision=highest)
    return (result[0], result[1])


def rotate(real_part, imag_part, cosine, sine, sign):
    return (
        real_part * cosine - sign * imag_part * sine,
        imag_part * cosine + sign * real_part * sine,
    )


def combine(mixed_re, mixed_im, grad_re, grad_im, filt_re, filt_im):
    conv_re = filt_re * mixed_re - filt_im * mixed_im
    conv_im = filt_re * mixed_im + filt_im * mixed_re
    corr_re = filt_re * grad_re + filt_im * grad_im
    corr_im = filt_re * grad_im - filt_im * grad_re
    cross_re = mixed_re * grad_re + mixed_im * grad_im
    cross_im = mixed_re * grad_im - mixed_im * grad_re
    return (conv_re - corr_im, conv_im + corr_re, cross_re, cross_im)


def featurize(extended, weights, row_count):
    tap_count = weights.shape[1]
    accumulated = jnp.zeros((row_count,) + extended.shape[1:], jnp.float32)
    for offset in range(tap_count):
        first_row = tap_count - 1 - offset
        accumulated = accumulated + weights[:, offset, :] * extended[
            first_row : first_row + row_count
        ].astype(jnp.float32)
    return accumulated


def transpose_pair(signals, filters):
    return (
        lax.all_to_all(signals, "seq", split_axis=0, concat_axis=1, tiled=True),
        lax.all_to_all(filters, "seq", split_axis=0, concat_axis=1, tiled=True),
    )


def sequence_plan(mixed_input, gated_grad, long_filter):
    row_count, chan_count = mixed_input.shape
    group_count = long_filter.shape[0]
    seq_count = lax.axis_size("seq")
    seq_index = lax.axis_index("seq")
    per_block = row_count // seq_count
    fft_length = 2 * row_count * seq_count
    freq_index = jnp.arange(2 * seq_count, dtype=jnp.int32)
    block_index = jnp.arange(seq_count, dtype=jnp.int32)
    row_index = jnp.arange(row_count, dtype=jnp.int32)
    signals = jnp.stack([mixed_input, gated_grad], 1)[:, None]
    filters = jnp.transpose(long_filter)[:, None]
    sig_cols, filt_cols = transpose_pair(signals, filters)
    cos_one, sin_one = angle_table(freq_index, block_index, 2 * seq_count)
    sig_re = einsum_high("kb,abxc->kaxc", cos_one, sig_cols)
    sig_im = -einsum_high("kb,abxc->kaxc", sin_one, sig_cols)
    filt_re = einsum_high("kb,abg->kag", cos_one, filt_cols)
    filt_im = -einsum_high("kb,abg->kag", sin_one, filt_cols)
    positions = seq_index * per_block + jnp.arange(per_block, dtype=jnp.int32)
    cos_twist, sin_twist = angle_table(freq_index, positions, fft_length)
    sig_re, sig_im = rotate(
        sig_re, sig_im, cos_twist[:, :, None, None], sin_twist[:, :, None, None], -1.0
    )
    filt_re, filt_im = rotate(filt_re, filt_im, cos_twist[:, :, None], sin_twist[:, :, None], -1.0)
    sig_rows, filt_rows = transpose_pair(
        jnp.stack([sig_re, sig_im], 2), jnp.stack([filt_re, filt_im], 2)
    )
    cos_two, sin_two = angle_table(row_index, row_index, row_count)
    spec_re, spec_im = complex_dft(
        cos_two, sin_two, sig_rows[:, :, 0], sig_rows[:, :, 1], "pqka,qjaxc->pjkxc", -1.0
    )
    hspec_re, hspec_im = complex_dft(
        cos_two, sin_two, filt_rows[:, :, 0], filt_rows[:, :, 1], "pqka,qjag->pjkg", -1.0
    )
    leading = spec_re.shape[:2]
    group_shape = leading + (group_count, chan_count // group_count)
    wave_re, wave_im, cross_re, cross_im = combine(
        spec_re[:, :, 0].reshape(group_shape),
        spec_im[:, :, 0].reshape(group_shape),
        spec_re[:, :, 1].reshape(group_shape),
        spec_im[:, :, 1].reshape(group_shape),
        hspec_re[..., None],
        hspec_im[..., None],
    )
    wave_re = wave_re.reshape(leading + (chan_count,))
    wave_im = wave_im.reshape(leading + (chan_count,))
    cross_re = jnp.sum(cross_re, -1)
    cross_im = jnp.sum(cross_im, -1)
    back_re, back_im = complex_dft(cos_two, sin_two, wave_re, wave_im, "pqak,qjkc->pajc", 1.0)
    cback_re, cback_im = complex_dft(cos_two, sin_two, cross_re, cross_im, "pqak,qjkg->pajg", 1.0)
    pair_freq = seq_index * 2 + jnp.arange(2, dtype=jnp.int32)
    cos_back, sin_back = angle_table(row_index, pair_freq, fft_length)
    back_re, back_im = rotate(back_re, back_im, cos_back[:, :, None], sin_back[:, :, None], 1.0)
    cback_re, cback_im = rotate(cback_re, cback_im, cos_back[:, :, None], sin_back[:, :, None], 1.0)
    wave_cols, cross_cols = transpose_pair(
        jnp.stack([back_re, back_im], 2), jnp.stack([cback_re, cback_im], 2)
    )
    cos_three, sin_three = angle_table(block_index, freq_index, 2 * seq_count)
    time_re, time_im = complex_dft(
        cos_three, sin_three, wave_cols[:, :, 0], wave_cols[:, :, 1], "pqbk,qakc->pbac", 1.0
    )
    cross_time = einsum_high("bk,akg->bag", cos_three, cross_cols[:, :, 0]) - einsum_high(
        "bk,akg->bag", sin_three, cross_cols[:, :, 1]
    )
    inverse_scale = 1.0 / fft_length
    wave_out, cross_out = transpose_pair(
        jnp.stack([time_re, time_im], 2) * inverse_scale, cross_time * inverse_scale
    )
    return (wave_out[0, :, 0], wave_out[0, :, 1], jnp.transpose(cross_out[0]))


def local(projected, cotangent, short_weight, long_filter):
    tap_count = short_weight.shape[1]
    row_count = projected.shape[0]
    margin = tap_count - 1
    front_rows = passed_along(projected[row_count - margin :], "seq", 1)
    extended = jnp.concatenate([front_rows, projected], 0)
    features = featurize(extended, short_weight, row_count)
    grad_out = cotangent.astype(jnp.float32)
    mixed_input = features[:, 1] * features[:, 2]
    gated_grad = grad_out * features[:, 0]
    conv_out, corr_out, filt_grad = sequence_plan(mixed_input, gated_grad, long_filter)
    token_count = row_count * lax.axis_size("seq")
    group_width = mixed_input.shape[1] // long_filter.shape[0]
    scaled_grad = filt_grad * (1.0 / math.sqrt(token_count * group_width))
    owned_grad = lax.all_to_all(scaled_grad, "ch", split_axis=1, concat_axis=0, tiled=True)
    feat_grad = jnp.stack(
        [grad_out * conv_out, corr_out * features[:, 2], corr_out * features[:, 1]], 1
    )
    next_rows = passed_along(feat_grad[:margin].astype(jnp.bfloat16), "seq", -1).astype(jnp.float32)
    extended_grad = jnp.concatenate([feat_grad, next_rows], 0)
    grad_proj = jnp.zeros(feat_grad.shape, jnp.float32)
    for offset in range(tap_count):
        grad_proj = (
            grad_proj + short_weight[:, offset, :] * extended_grad[offset : offset + row_count]
        )
    short_terms = []
    for offset in range(tap_count):
        first_row = margin - offset
        short_terms.append(
            jnp.sum(feat_grad * extended[first_row : first_row + row_count].astype(jnp.float32), 0)
        )
    grad_short = lax.psum(jnp.stack(short_terms, 1), "seq") * (1.0 / math.sqrt(token_count))
    return (grad_proj.astype(jnp.bfloat16), grad_short, owned_grad)


def solution(mesh):
    return jax.shard_map(
        local,
        mesh=mesh,
        in_specs=(P("seq", None, "ch"), P("seq", "ch"), P(None, None, "ch"), P("ch", "seq")),
        out_specs=(P("seq", None, "ch"), P(None, None, "ch"), P(None, ("seq", "ch"))),
        check_vma=False,
    )
```

profile of v0, /device:TPU:16, one launch (start us, length us, event | category | flops | bytes accessed | tf_op | source)
XLA Modules:
  0.0 929.5 jit_solution(14938506437671617002)
XLA Ops:
  8.1 3.8 collective-permute-start
  13.4 11.8 %all-to-all-start = ((f32[128,1,2]{2,1,0:T(1,128)}), f32[128,1,2]{2,1,0:T(1,128)S(1)}, u32[]{:S(2)}, u32[]{:S(2)}) async-start(f32[128,1,2]{2,1,0:T(1,128)} %bitcast.9), calls=%async_computation | async-start | bytes 131072 | tf_op jit(solution)/shard_map/all_to_all | solution.py:66
  28.6 5.6 fusion.9
  38.0 11.2 %all-to-all-start.2 = ((f32[128,1,2,1024]{3,2,1,0:T(2,128)}), f32[128,1,2,1024]{3,2,1,0:T(2,128)S(1)}, u32[]{:S(2)}, u32[]{:S(2)}) async-start(f32[128,1,2,1024]{3,2,1,0:T(2,128)} %copy.147), calls=%async_computation.2 | async-start | bytes 2097152 | tf_op jit(solution)/shard_map/all_to_all | solution.py:65
  51.5 25.5 %all-to-all-done.2 = f32[128,1,2,1024]{3,2,1,0:T(2,128)S(1)} async-done(((f32[128,1,2,1024]{3,2,1,0:T(2,128)}), f32[128,1,2,1024]{3,2,1,0:T(2,128)S(1)}, u32[]{:S(2)}, u32[]{:S(2)}) %all-to-all-start.2) | async-done | bytes 1048608 | tf_op jit(solution)/shard_map/all_to_all | solution.py:65
  77.1 6.5 all-to-all-start.1
  89.4 5.2 copy.149
  95.8 10.6 %all-to-all-start.3 = ((f32[128,2,2,2,1024]{4,3,1,2,0:T(2,128)}), f32[128,2,2,2,1024]{4,3,1,2,0:T(2,128)}, u32[]{:S(2)}, u32[]{:S(2)}) async-start(f32[128,2,2,2,1024]{4,3,1,2,0:T(2,128)} %copy.149), calls=%async_computation.3 | async-start | bytes 8388608 | tf_op jit(solution)/shard_map/all_to_all | solution.py:65
  110.6 88.6 %all-to-all-done.3 = f32[128,2,2,2,1024]{4,3,1,2,0:T(2,128)} async-done(((f32[128,2,2,2,1024]{4,3,1,2,0:T(2,128)}), f32[128,2,2,2,1024]{4,3,1,2,0:T(2,128)}, u32[]{:S(2)}, u32[]{:S(2)}) %all-to-all-start.3) | async-done | bytes 4194336 | tf_op jit(solution)/shard_map/all_to_all | solution.py:65
  199.2 4.2 copy.150
  209.8 4.1 copy.213
  213.9 5.1 fusion.3
  229.8 8.1 all-to-all-start.6
  242.2 7.7 all-to-all-done.6
  255.5 4.6 all-to-all-start.7
  263.3 7.4 all-to-all-done.7
  270.8 4.7 all-to-all-start.4
  276.8 44.4 %all-to-all-done.4 = f32[128,2,2,1024]{3,1,2,0:T(2,128)S(1)} async-done(((f32[128,2,2,1024]{3,1,2,0:T(2,128)}), f32[128,2,2,1024]{3,1,2,0:T(2,128)S(1)}, u32[]{:S(2)}, u32[]{:S(2)}) %all-to-all-start.4) | async-done | bytes 2097184 | tf_op jit(solution)/shard_map/all_to_all | solution.py:65
  321.2 5.0 all-to-all-start.8
  334.5 6.7 all-to-all-start.5
  341.2 29.2 %all-to-all-done.5 = f32[64,2,2,1024]{3,1,2,0:T(2,128)S(1)} async-done(((f32[64,2,2,1024]{3,1,2,0:T(2,128)}), f32[64,2,2,1024]{3,1,2,0:T(2,128)S(1)}, u32[]{:S(2)}, u32[]{:S(2)}) %all-to-all-start.5) | async-done | bytes 1048608 | tf_op jit(solution)/shard_map/all_to_all | solution.py:65
  375.9 5.4 fusion.16
  390.2 3.8 fusion.18
  395.2 525.0 %all-reduce.2.cloned.1.call-done = f32[3,7,1024]{2,0,1:T(4,128)} async-done(((f32[3,7,1024]{2,0,1:T(4,128)}), f32[3,7,1024]{2,0,1:T(4,128)}) %all-reduce.2.cloned.1.call-update) | async-done | bytes 86032 | tf_op jit(solution)/shard_map/psum | solution.py:172
  (139 shorter events, 80.5 us)
Async XLA Ops:
  7.2 21.5 %copy-start.2 = (bf16[128,3,1024]{2,0,1:T(8,128)(2,1)S(1)}, bf16[128,3,1024]{2,0,1:T(8,128)(2,1)}, u32[]{:S(2)}) copy-start(bf16[128,3,1024]{2,0,1:T(8,128)(2,1)} %param.4) | copy-start | bytes 2359300
  8.1 18.6 %collective-permute-start = (bf16[6,3,1024]{2,1,0:T(4,128)(2,1)S(1)}, bf16[6,3,1024]{2,1,0:T(4,128)(2,1)S(1)}, u32[]{:S(2)}, u32[]{:S(2)}) collective-permute-start(bf16[6,3,1024]{2,1,0:T(4,128)(2,1)S(1)} %copy.248), channel_id=1, source_target_pairs={{0,4},{4,8},{8,12},{12,16},{16,20},{20,24},{24,28},{28,32},{32,36}... | collective-permute-start | bytes 110600 | tf_op jit(solution)/shard_map/ppermute | solution.py:13
  13.4 24.6 %all-to-all-start = ((f32[128,1,2]{2,1,0:T(1,128)}), f32[128,1,2]{2,1,0:T(1,128)S(1)}, u32[]{:S(2)}, u32[]{:S(2)}) async-start(f32[128,1,2]{2,1,0:T(1,128)} %bitcast.9), calls=%async_computation | async-start | bytes 131072 | tf_op jit(solution)/shard_map/all_to_all | solution.py:66
  26.7 7.6 copy-start.11
  34.3 1.4 copy-start.1
  34.3 1.4 copy-start.8
  38.0 39.1 %all-to-all-start.2 = ((f32[128,1,2,1024]{3,2,1,0:T(2,128)}), f32[128,1,2,1024]{3,2,1,0:T(2,128)S(1)}, u32[]{:S(2)}, u32[]{:S(2)}) async-start(f32[128,1,2,1024]{3,2,1,0:T(2,128)} %copy.147), calls=%async_computation.2 | async-start | bytes 2097152 | tf_op jit(solution)/shard_map/all_to_all | solution.py:65
  50.0 36.0 %copy-start.13 = (f32[128,2]{0,1:T(2,128)}, f32[128,2]{0,1:T(2,128)S(1)}, u32[]{:S(2)}) copy-start(f32[128,2]{0,1:T(2,128)S(1)} %get-tuple-element.73) | copy-start | bytes 3076
  77.1 18.8 %all-to-all-start.1 = ((f32[128,2,2,2]{3,1,2,0:T(2,128)}), f32[128,2,2,2]{3,1,2,0:T(2,128)S(1)}, u32[]{:S(2)}, u32[]{:S(2)}) async-start(f32[128,2,2,2]{3,1,2,0:T(2,128)} %copy.137), calls=%async_computation.1 | async-start | bytes 524288 | tf_op jit(solution)/shard_map/all_to_all | solution.py:66
  95.8 103.3 %all-to-all-start.3 = ((f32[128,2,2,2,1024]{4,3,1,2,0:T(2,128)}), f32[128,2,2,2,1024]{4,3,1,2,0:T(2,128)}, u32[]{:S(2)}, u32[]{:S(2)}) async-start(f32[128,2,2,2,1024]{4,3,1,2,0:T(2,128)} %copy.149), calls=%async_computation.3 | async-start | bytes 8388608 | tf_op jit(solution)/shard_map/all_to_all | solution.py:65
  222.2 3.8 copy-start.6
  222.2 3.8 copy-start.7
  229.8 20.1 %all-to-all-start.6 = ((f32[128,2,2,2]{3,1,2,0:T(2,128)}), f32[128,2,2,2]{3,1,2,0:T(2,128)}, u32[]{:S(2)}, u32[]{:S(2)}) async-start(f32[128,2,2,2]{3,1,2,0:T(2,128)} %copy.168), calls=%async_computation.6 | async-start | bytes 524288 | tf_op jit(solution)/shard_map/all_to_all | solution.py:66
  239.9 2.0 copy-start.14
  239.9 2.0 copy-start.15
  255.5 15.3 %all-to-all-start.7 = ((f32[64,2,2]{2,1,0:T(2,128)}), f32[64,2,2]{2,1,0:T(2,128)S(1)}, u32[]{:S(2)}, u32[]{:S(2)}) async-start(f32[64,2,2]{2,1,0:T(2,128)} %copy.173), calls=%async_computation.7 | async-start | bytes 131072 | tf_op jit(solution)/shard_map/all_to_all | solution.py:66
  270.8 50.4 %all-to-all-start.4 = ((f32[128,2,2,1024]{3,1,2,0:T(2,128)}), f32[128,2,2,1024]{3,1,2,0:T(2,128)S(1)}, u32[]{:S(2)}, u32[]{:S(2)}) async-start(f32[128,2,2,1024]{3,1,2,0:T(2,128)} %copy.156), calls=%async_computation.4 | async-start | bytes 4194304 | tf_op jit(solution)/shard_map/all_to_all | solution.py:65
  321.2 13.3 %all-to-all-start.8 = ((f32[2,4,32]{2,0,1:T(2,128)}), f32[2,4,32]{2,0,1:T(2,128)S(1)}, u32[]{:S(2)}, u32[]{:S(2)}) async-start(f32[2,4,32]{2,0,1:T(2,128)} %copy.176), calls=%async_computation.8 | async-start | bytes 8192 | tf_op jit(solution)/shard_map/all_to_all | solution.py:155
  334.5 35.9 %all-to-all-start.5 = ((f32[64,2,2,1024]{3,1,2,0:T(2,128)}), f32[64,2,2,1024]{3,1,2,0:T(2,128)S(1)}, u32[]{:S(2)}, u32[]{:S(2)}) async-start(f32[64,2,2,1024]{3,1,2,0:T(2,128)} %copy.159), calls=%async_computation.5 | async-start | bytes 2097152 | tf_op jit(solution)/shard_map/all_to_all | solution.py:65
  341.1 579.1 %all-reduce.2.cloned.1.call-start = ((), (), s32[]{:S(2)}) async-start(), calls=%async_computation.9 | async-start | bytes 229376 | tf_op jit(solution)/shard_map/psum | solution.py:172
  370.9 3.5 copy-start.5
  371.8 3.4 copy-start.9
  382.8 6.0 collective-permute-start.1
  384.3 5.9 copy-start.12
  (4 other events, 4.1 us)
Sparse Core Ops, SparseCore 0:
  385.2 534.9 all-reduce.1
where the time goes:
time: 937 us; the launch traced here: 929 us
  waiting for transfers between devices  733 us (78%)
  starting transfers between devices  74.5 us (8%)
  local copies, waits for them, and re-layouts  57.2 us (6%)
  other arithmetic  34.2 us (4%)
  matrix products  16 us (2%)
  between operations  15 us (2%)
    psum x1, waiting for transfers between devices, local(): lax.psum(jnp.stack(short_terms, 1), 'seq') * (1.0 / math.sqrt(token_count))  525 us
    all_to_all x4, waiting for transfers between devices, transpose_pair(): lax.all_to_all(signals, 'seq', split_axis=0, concat_axis=1, tiled=True)  188 us
    all_to_all x4, starting transfers between devices, transpose_pair(): lax.all_to_all(signals, 'seq', split_axis=0, concat_axis=1, tiled=True)  33.2 us
    all_to_all x4, starting transfers between devices, transpose_pair(): lax.all_to_all(filters, 'seq', split_axis=0, concat_axis=1, tiled=True)  30.9 us
  transfers between devices with their start and end apart: 12, of which 9 were waited for; matrix products, arithmetic and copies ran while one was open for 6% of the time, Pallas kernels for 0%

commit v1 on v0

--- a/solution.py
+++ b/solution.py
@@ -5,6 +5,12 @@
 from jax.sharding import PartitionSpec as P
 
 highest = lax.Precision.HIGHEST
+
+
+def gather_and_add(shard, name):
+    parts = lax.all_gather(shard, name, axis=0, tiled=False)
+    total = parts.sum(axis=0)
+    return total
 
 
 def passed_along(block, axis, distance):
@@ -169,7 +175,7 @@
         short_terms.append(
             jnp.sum(feat_grad * extended[first_row : first_row + row_count].astype(jnp.float32), 0)
         )
-    grad_short = lax.psum(jnp.stack(short_terms, 1), "seq") * (1.0 / math.sqrt(token_count))
+    grad_short = gather_and_add(jnp.stack(short_terms, 1), "seq") * (1.0 / math.sqrt(token_count))
     return (grad_proj.astype(jnp.bfloat16), grad_short, owned_grad)
 
 

time: 937 us -> 662 us (0.71)
  waiting for transfers between devices: 733 us -> 406 us
  blocking collectives: 0 us -> 73.9 us
  starting transfers between devices: 74.5 us -> 53 us
    psum x1 -> x0, waiting for transfers between devices: 525 us -> none  [local(): lax.psum(jnp.stack(short_terms, 1), 'seq') * (1.0 / math.sqrt(token_count))]
    all_gather x0 -> x1, waiting for transfers between devices: none -> 243 us  [gather_and_add(): parts = lax.all_gather(shard, name, axis=0, tiled=False)]
    all_to_all x0 -> x4, blocking collectives: none -> 73.9 us  [the longest x2 35.4 us: transpose_pair(): lax.all_to_all(filters, 'seq', split_axis=0, concat_axis=1, tiled=True)]
    all_to_all x4 -> x3, waiting for transfers between devices: 188 us -> 162 us  [transpose_pair(): lax.all_to_all(signals, 'seq', split_axis=0, concat_axis=1, tiled=True)]
    all_to_all x4 -> x2, waiting for transfers between devices: 16.3 us -> 1.14 us  [transpose_pair(): lax.all_to_all(filters, 'seq', split_axis=0, concat_axis=1, tiled=True)]
    all_to_all x4 -> x2, starting transfers between devices: 30.9 us -> 18.2 us  [transpose_pair(): lax.all_to_all(filters, 'seq', split_axis=0, concat_axis=1, tiled=True)]
    all_to_all x4 -> x3, starting transfers between devices: 33.2 us -> 29.4 us  [transpose_pair(): lax.all_to_all(signals, 'seq', split_axis=0, concat_axis=1, tiled=True)]
  transfers between devices with their start and end apart: 12 -> 8, of which waited for: 9 -> 5; matrix products, arithmetic and copies ran while one was open for 6% -> 7% of each run, Pallas kernels for 0% -> 0%
where the time goes in v1:
time: 662 us; the launch traced here: 654 us
  waiting for transfers between devices  406 us (61%)
  blocking collectives  73.9 us (11%)
  local copies, waits for them, and re-layouts  55.5 us (8%)
  starting transfers between devices  53 us (8%)
  other arithmetic  35 us (5%)
  matrix products  15.3 us (2%)
  between operations  15.2 us (2%)
    all_gather x1, waiting for transfers between devices, gather_and_add(): parts = lax.all_gather(shard, name, axis=0, tiled=False)  243 us
    all_to_all x3, waiting for transfers between devices, transpose_pair(): lax.all_to_all(signals, 'seq', split_axis=0, concat_axis=1, tiled=True)  162 us
    all_to_all x2, blocking collectives, transpose_pair(): lax.all_to_all(filters, 'seq', split_axis=0, concat_axis=1, tiled=True)  35.4 us
    all_to_all x1, blocking collectives, transpose_pair(): lax.all_to_all(signals, 'seq', split_axis=0, concat_axis=1, tiled=True)  31.9 us
    all_to_all x3, starting transfers between devices, transpose_pair(): lax.all_to_all(signals, 'seq', split_axis=0, concat_axis=1, tiled=True)  29.4 us
    all_to_all x2, starting transfers between devices, transpose_pair(): lax.all_to_all(filters, 'seq', split_axis=0, concat_axis=1, tiled=True)  18.2 us
  transfers between devices with their start and end apart: 8, of which 5 were waited for; matrix products, arithmetic and copies ran while one was open for 7% of the time, Pallas kernels for 0%

profile of v1, /device:TPU:16, one launch (start us, length us, event | category | flops | bytes accessed | tf_op | source)
XLA Modules:
  0.0 654.1 jit_solution(13811315159614352652)
XLA Ops:
  8.1 3.8 collective-permute-start
  13.4 11.8 %all-to-all-start = ((f32[128,1,2]{2,1,0:T(1,128)}), f32[128,1,2]{2,1,0:T(1,128)S(1)}, u32[]{:S(2)}, u32[]{:S(2)}) async-start(f32[128,1,2]{2,1,0:T(1,128)} %bitcast.9), calls=%async_computation | async-start | bytes 131072 | tf_op jit(solution)/shard_map/all_to_all | solution.py:72
  28.7 5.6 fusion.9
  38.0 11.2 %all-to-all-start.2 = ((f32[128,1,2,1024]{3,2,1,0:T(2,128)}), f32[128,1,2,1024]{3,2,1,0:T(2,128)S(1)}, u32[]{:S(2)}, u32[]{:S(2)}) async-start(f32[128,1,2,1024]{3,2,1,0:T(2,128)} %copy.144), calls=%async_computation.2 | async-start | bytes 2097152 | tf_op jit(solution)/shard_map/all_to_all | solution.py:71
  51.0 26.1 %all-to-all-done.2 = f32[128,1,2,1024]{3,2,1,0:T(2,128)S(1)} async-done(((f32[128,1,2,1024]{3,2,1,0:T(2,128)}), f32[128,1,2,1024]{3,2,1,0:T(2,128)S(1)}, u32[]{:S(2)}, u32[]{:S(2)}) %all-to-all-start.2) | async-done | bytes 1048608 | tf_op jit(solution)/shard_map/all_to_all | solution.py:71
  77.1 6.5 all-to-all-start.1
  89.5 5.3 copy.146
  95.9 10.5 %all-to-all-start.3 = ((f32[128,2,2,2,1024]{4,3,1,2,0:T(2,128)}), f32[128,2,2,2,1024]{4,3,1,2,0:T(2,128)}, u32[]{:S(2)}, u32[]{:S(2)}) async-start(f32[128,2,2,2,1024]{4,3,1,2,0:T(2,128)} %copy.146), calls=%async_computation.3 | async-start | bytes 8388608 | tf_op jit(solution)/shard_map/all_to_all | solution.py:71
  109.9 89.2 %all-to-all-done.3 = f32[128,2,2,2,1024]{4,3,1,2,0:T(2,128)} async-done(((f32[128,2,2,2,1024]{4,3,1,2,0:T(2,128)}), f32[128,2,2,2,1024]{4,3,1,2,0:T(2,128)}, u32[]{:S(2)}, u32[]{:S(2)}) %all-to-all-start.3) | async-done | bytes 4194336 | tf_op jit(solution)/shard_map/all_to_all | solution.py:71
  199.1 4.2 copy.147
  203.3 3.7 fusion.141
  209.7 4.5 copy.209
  214.2 5.1 fusion.3
  227.5 7.7 %all-to-all-start.4 = ((f32[128,2,2,1024]{3,1,2,0:T(2,128)}), f32[128,2,2,1024]{3,1,2,0:T(2,128)}, u32[]{:S(2)}, u32[]{:S(2)}) async-start(f32[128,2,2,1024]{3,1,2,0:T(2,128)} %copy.153), calls=%async_computation.4 | async-start | bytes 4194304 | tf_op jit(solution)/shard_map/all_to_all | solution.py:71
  236.2 47.0 %all-to-all-done.4 = f32[128,2,2,1024]{3,1,2,0:T(2,128)} async-done(((f32[128,2,2,1024]{3,1,2,0:T(2,128)}), f32[128,2,2,1024]{3,1,2,0:T(2,128)}, u32[]{:S(2)}, u32[]{:S(2)}) %all-to-all-start.4) | async-done | bytes 2097184 | tf_op jit(solution)/shard_map/all_to_all | solution.py:71
  283.1 3.7 copy.248
  286.9 3.8 all_to_all.127
  294.6 31.9 %all_to_all.148 = f32[64,2,2,1024]{3,1,2,0:T(2,128)S(1)} all-to-all(f32[64,2,2,1024]{3,1,2,0:T(2,128)S(1)} %copy.156), channel_id=1, replica_groups=mesh['seq'=64,'ch'=4] {'seq'}, dimensions={0} | all-to-all | bytes 2097152 | tf_op jit(solution)/shard_map/all_to_all | solution.py:71
  332.1 5.3 fusion.16
  344.8 18.8 %all_to_all.149 = f32[128,2,2,2]{3,1,2,0:T(2,128)S(1)} all-to-all(f32[128,2,2,2]{3,1,2,0:T(2,128)S(1)} %copy.165), channel_id=1, replica_groups=mesh['seq'=64,'ch'=4] {'seq'}, dimensions={0} | all-to-all | bytes 8192 | tf_op jit(solution)/shard_map/all_to_all | solution.py:72
  366.3 16.7 %all_to_all.150 = f32[64,2,2]{2,1,0:T(2,128)S(1)} all-to-all(f32[64,2,2]{2,1,0:T(2,128)S(1)} %copy.170), channel_id=1, replica_groups=mesh['seq'=64,'ch'=4] {'seq'}, dimensions={0} | all-to-all | bytes 2048 | tf_op jit(solution)/shard_map/all_to_all | solution.py:72
  386.4 6.6 %all_to_all.151 = f32[2,4,32]{2,0,1:T(2,128)S(1)} all-to-all(f32[2,4,32]{2,0,1:T(2,128)S(1)} %copy.173), channel_id=1, replica_groups=mesh['seq'=64,'ch'=4] {'ch'}, dimensions={1} | all-to-all | bytes 2048 | tf_op jit(solution)/shard_map/all_to_all | solution.py:161
  394.5 3.8 fusion.18
  399.5 242.9 %all-gather.3.cloned.1.call-done = f32[192,7,1024]{2,1,0:T(8,128)} async-done(((f32[3,7,1024]{2,1,0:T(8,128)}), f32[192,7,1024]{2,1,0:T(8,128)}) %all-gather.3.cloned.1.call-update) | async-done | bytes 5505040 | tf_op jit(solution)/shard_map/all_gather | solution.py:11
  (166 shorter events, 63.4 us)
Async XLA Ops:
  7.2 21.5 %copy-start.8 = (bf16[128,3,1024]{2,0,1:T(8,128)(2,1)S(1)}, bf16[128,3,1024]{2,0,1:T(8,128)(2,1)}, u32[]{:S(2)}) copy-start(bf16[128,3,1024]{2,0,1:T(8,128)(2,1)} %param.4) | copy-start | bytes 2359300
  8.1 18.6 %collective-permute-start = (bf16[6,3,1024]{2,1,0:T(4,128)(2,1)S(1)}, bf16[6,3,1024]{2,1,0:T(4,128)(2,1)S(1)}, u32[]{:S(2)}, u32[]{:S(2)}) collective-permute-start(bf16[6,3,1024]{2,1,0:T(4,128)(2,1)S(1)} %copy.244), channel_id=1, source_target_pairs={{0,4},{4,8},{8,12},{12,16},{16,20},{20,24},{24,28},{28,32},{32,36}... | collective-permute-start | bytes 110600 | tf_op jit(solution)/shard_map/ppermute | solution.py:19
  13.4 24.7 %all-to-all-start = ((f32[128,1,2]{2,1,0:T(1,128)}), f32[128,1,2]{2,1,0:T(1,128)S(1)}, u32[]{:S(2)}, u32[]{:S(2)}) async-start(f32[128,1,2]{2,1,0:T(1,128)} %bitcast.9), calls=%async_computation | async-start | bytes 131072 | tf_op jit(solution)/shard_map/all_to_all | solution.py:72
  26.7 7.6 %copy-start.17 = (f32[3,1024]{1,0:T(4,128)}, f32[3,1024]{1,0:T(4,128)S(1)}, u32[]{:S(2)}) copy-start(f32[3,1024]{1,0:T(4,128)S(1)} %get-tuple-element.76) | copy-start | bytes 36868
  26.7 7.6 %copy-start.19 = (f32[3,1024]{1,0:T(4,128)}, f32[3,1024]{1,0:T(4,128)S(1)}, u32[]{:S(2)}) copy-start(f32[3,1024]{1,0:T(4,128)S(1)} %get-tuple-element.77) | copy-start | bytes 36868
  26.7 7.6 %copy-start.21 = (f32[3,1024]{1,0:T(4,128)}, f32[3,1024]{1,0:T(4,128)S(1)}, u32[]{:S(2)}) copy-start(f32[3,1024]{1,0:T(4,128)S(1)} %get-tuple-element.74) | copy-start | bytes 36868
  26.7 7.6 %copy-start.23 = (f32[3,1024]{1,0:T(4,128)}, f32[3,1024]{1,0:T(4,128)S(1)}, u32[]{:S(2)}) copy-start(f32[3,1024]{1,0:T(4,128)S(1)} %get-tuple-element.75) | copy-start | bytes 36868
  26.7 7.6 %copy-start.25 = (f32[3,1,1024]{2,0,1:T(4,128)}, f32[3,1,1024]{2,0,1:T(4,128)S(1)}, u32[]{:S(2)}) copy-start(f32[3,1,1024]{2,0,1:T(4,128)S(1)} %copy.249) | copy-start | bytes 36868
  38.0 39.1 %all-to-all-start.2 = ((f32[128,1,2,1024]{3,2,1,0:T(2,128)}), f32[128,1,2,1024]{3,2,1,0:T(2,128)S(1)}, u32[]{:S(2)}, u32[]{:S(2)}) async-start(f32[128,1,2,1024]{3,2,1,0:T(2,128)} %copy.144), calls=%async_computation.2 | async-start | bytes 2097152 | tf_op jit(solution)/shard_map/all_to_all | solution.py:71
  49.4 174.5 %copy-start.27 = (f32[128,2]{0,1:T(2,128)}, f32[128,2]{0,1:T(2,128)S(1)}, u32[]{:S(2)}) copy-start(f32[128,2]{0,1:T(2,128)S(1)} %get-tuple-element.73) | copy-start | bytes 3076
  49.4 174.5 %copy-start.29 = (f32[128,2]{0,1:T(2,128)}, f32[128,2]{0,1:T(2,128)S(1)}, u32[]{:S(2)}) copy-start(f32[128,2]{0,1:T(2,128)S(1)} %get-tuple-element.71) | copy-start | bytes 3076
  77.1 18.8 %all-to-all-start.1 = ((f32[128,2,2,2]{3,1,2,0:T(2,128)}), f32[128,2,2,2]{3,1,2,0:T(2,128)S(1)}, u32[]{:S(2)}, u32[]{:S(2)}) async-start(f32[128,2,2,2]{3,1,2,0:T(2,128)} %copy.134), calls=%async_computation.1 | async-start | bytes 524288 | tf_op jit(solution)/shard_map/all_to_all | solution.py:72
  95.9 103.2 %all-to-all-start.3 = ((f32[128,2,2,2,1024]{4,3,1,2,0:T(2,128)}), f32[128,2,2,2,1024]{4,3,1,2,0:T(2,128)}, u32[]{:S(2)}, u32[]{:S(2)}) async-start(f32[128,2,2,2,1024]{4,3,1,2,0:T(2,128)} %copy.146), calls=%async_computation.3 | async-start | bytes 8388608 | tf_op jit(solution)/shard_map/all_to_all | solution.py:71
  227.5 55.7 %all-to-all-start.4 = ((f32[128,2,2,1024]{3,1,2,0:T(2,128)}), f32[128,2,2,1024]{3,1,2,0:T(2,128)}, u32[]{:S(2)}, u32[]{:S(2)}) async-start(f32[128,2,2,1024]{3,1,2,0:T(2,128)} %copy.153), calls=%async_computation.4 | async-start | bytes 4194304 | tf_op jit(solution)/shard_map/all_to_all | solution.py:71
  235.2 407.2 %all-gather.3.cloned.1.call-start = ((), (), s32[]{:S(2)}) async-start(), calls=%async_computation.9 | async-start | bytes 6389760 | tf_op jit(solution)/shard_map/all_gather | solution.py:11
  341.5 41.6 %copy-start.2 = (f32[128,1,1024]{2,1,0:T(1,128)S(1)}, f32[128,1,1024]{2,1,0:T(1,128)}, u32[]{:S(2)}) copy-start(f32[128,1,1024]{2,1,0:T(1,128)} %copy-done.1) | copy-start | bytes 1572868
  341.5 41.6 %copy-start.4 = (f32[128,1,1024]{2,1,0:T(1,128)S(1)}, f32[128,1,1024]{2,1,0:T(1,128)}, u32[]{:S(2)}) copy-start(f32[128,1,1024]{2,1,0:T(1,128)} %copy-done.3) | copy-start | bytes 1572868
  341.5 41.6 %copy-start.6 = (f32[128,1,1024]{2,1,0:T(1,128)S(1)}, f32[128,1,1024]{2,1,0:T(1,128)}, u32[]{:S(2)}) copy-start(f32[128,1,1024]{2,1,0:T(1,128)} %copy-done.5) | copy-start | bytes 1572868
  384.6 9.9 %copy-start.18 = (f32[3,1024]{1,0:T(4,128)S(1)}, f32[3,1024]{1,0:T(4,128)}, u32[]{:S(2)}) copy-start(f32[3,1024]{1,0:T(4,128)} %copy-done.17) | copy-start | bytes 36868
  384.6 9.9 %copy-start.20 = (f32[3,1024]{1,0:T(4,128)S(1)}, f32[3,1024]{1,0:T(4,128)}, u32[]{:S(2)}) copy-start(f32[3,1024]{1,0:T(4,128)} %copy-done.19) | copy-start | bytes 36868
  384.6 9.9 %copy-start.22 = (f32[3,1024]{1,0:T(4,128)S(1)}, f32[3,1024]{1,0:T(4,128)}, u32[]{:S(2)}) copy-start(f32[3,1024]{1,0:T(4,128)} %copy-done.21) | copy-start | bytes 36868
  384.6 9.9 %copy-start.24 = (f32[3,1024]{1,0:T(4,128)S(1)}, f32[3,1024]{1,0:T(4,128)}, u32[]{:S(2)}) copy-start(f32[3,1024]{1,0:T(4,128)} %copy-done.23) | copy-start | bytes 36868
  384.7 9.9 %copy-start.26 = (f32[3,1,1024]{2,0,1:T(4,128)S(1)}, f32[3,1,1024]{2,0,1:T(4,128)}, u32[]{:S(2)}) copy-start(f32[3,1,1024]{2,0,1:T(4,128)} %copy-done.25) | copy-start | bytes 36868
  384.7 8.4 %collective-permute-start.1 = (bf16[6,3,1024]{2,1,0:T(4,128)(2,1)S(1)}, bf16[6,3,1024]{2,1,0:T(4,128)(2,1)S(1)}, u32[]{:S(2)}, u32[]{:S(2)}) collective-permute-start(bf16[6,3,1024]{2,1,0:T(4,128)(2,1)S(1)} %slice.341), channel_id=1, source_target_pairs={{4,0},{8,4},{12,8},{16,12},{20,16},{24,20},{28,24},{32,28},{36,32}... | collective-permute-start | bytes 110600 | tf_op jit(solution)/shard_map/ppermute | solution.py:19
  (15 other events, 35.8 us)
Sparse Core Ops, SparseCore 0:
  338.5 303.8 all-gather.2
